TPU v7x, 128 devices: a whole 4x4x4 slice. The times are simulated.
128 devices in a mesh: tgt: 16 (over z_lo, y, core), src: 8 (over x, z_hi).
Axes of the slice: x: 4, y: 4, z: 4 (z_hi: 2, z_lo: 2; z = z_hi * 2 + z_lo), core: 2. Of those that a mesh axis runs over, the one named last changes fastest.
Arguments:
- targets: float32 [16, 64, 4096], P('tgt'), may hold values from -8 to 8
- sources: float32 [16, 64, 4096], P('src', 'tgt'), may hold values from -8 to 8
- occupations: float32 [16], P('src'), may hold values from 0.2 to 2
Outputs:
- exchange_term: float32 [16, 64, 4096], P('tgt', 'src')
All inputs are finite; a program needn't handle non-finite values.
Results may differ from a plain program's by a relative error of at most 0.000076.
Values sent between devices are 32-bit elements; how exact they have to be, the bound alone decides.
No kernel may reach another device: no remote copies, remote signals or barrier semaphores. Data moves between devices by JAX's collectives and lax.ppermute only.
A program may use at most 64 MiB of HBM per device.

v0:
```python
import jax
import jax.numpy as jnp
import numpy as np
from jax import lax
from jax.experimental import pallas as pl
from jax.experimental.pallas import tpu as pltpu
from jax.sharding import PartitionSpec as P

N = 64
H = 32
L = 128
PITCH = N + 2
BLOCK = 16
CHUNK = 2 * H * 4
SLAB = H * 8
EARLY = 10


def real_basis():
    n = np.arange(N)
    rows = [np.ones(N)]
    for k in range(1, N // 2):
        rows.append(np.sqrt(2.0) * np.cos(2 * np.pi * k * n / N))
    rows.append((-1.0) ** n)
    for k in range(1, N // 2):
        rows.append(np.sqrt(2.0) * np.sin(2 * np.pi * k * n / N))
    freq = np.array(list(range(0, N // 2 + 1)) + list(range(1, N // 2)), np.float64)
    return np.array(rows) / np.sqrt(N), freq


def halves(table):
    high = table.astype(jnp.bfloat16)
    low = (table - high.astype(np.float64)).astype(jnp.bfloat16)
    return high, low


def left_table(matrix):
    high, low = halves(matrix)
    return np.concatenate([high, high, low], axis=1)


def right_table(matrix):
    block = np.zeros((L, L))
    block[:N, :N] = matrix
    block[N:, N:] = matrix
    high, low = halves(block)
    both = np.concatenate([high, low], axis=1)
    return np.concatenate([both, both], axis=0)


BASIS, _ = real_basis()
ORDER = np.concatenate([np.arange(0, N, 2), np.arange(1, N, 2)])
BASIS_Y = BASIS[:, ORDER]


def split(value):
    high = value.astype(jnp.bfloat16)
    low = (value - high.astype(jnp.float32)).astype(jnp.bfloat16)
    return high, low


def dot(left, right):
    return jnp.dot(left, right, preferred_element_type=jnp.float32)


def stacked(value):
    high, low = split(value)
    return jnp.concatenate([high, low, high], axis=0)


def from_left(table, first, second):
    out = dot(table, jnp.concatenate([stacked(first), stacked(second)], axis=1))
    return out[:, :L], out[:, L:]


def from_right(value, table):
    high, low = split(value)
    out = dot(jnp.concatenate([high, low], axis=1), table)
    return out[:, :L] + out[:, L:]


def pipelined(first, second, count, buffers):
    first(0, buffers[0])
    for n in range(1, count):
        first(n, buffers[n % 2])
        second(n - 1, buffers[(n - 1) % 2])
    second(count - 1, buffers[(count - 1) % 2])


def lane_mask():
    return lax.broadcasted_iota(jnp.int32, (H, L), 1) < N


def mixed(first, second, lane):
    low = jnp.where(lane, first, pltpu.roll(second, N, axis=1))
    high = jnp.where(lane, pltpu.roll(first, N, axis=1), second)
    return low, high


def near_transforms(chunks, starts, t_in, s_ref, one, refs, after=None):
    chunk_ref, t_ref, sems, held, ly, rz = refs
    lane = lane_mask()
    count = len(starts) // 2
    copies = []
    for n in range(count):
        group = pl.ds(pl.multiple_of(starts[2 * n] // 8 * SLAB, SLAB), SLAB)
        wanted = [
            pltpu.make_async_copy(t_in.at[group], t_ref.at[pl.ds(n * SLAB, SLAB)], sems.at[3 * n])
        ]
        for e in range(2):
            c = 2 * n + e
            wanted.append(
                pltpu.make_async_copy(
                    chunks[c], chunk_ref.at[pl.ds(c * CHUNK, CHUNK)], sems.at[3 * n + 1 + e]
                )
            )
        for copy in wanted:
            copy.start()
        copies.append(wanted)

    def depth(n, buffer):
        for copy in copies[n]:
            copy.wait()
        planes = []
        for c in range(2 * n, 2 * n + 2):
            within = starts[c] % 8
            for e in range(4):
                a = chunk_ref[pl.ds(c * CHUNK + e, H, stride=4), :]
                b = chunk_ref[pl.ds(c * CHUNK + CHUNK // 2 + e, H, stride=4), :]
                low, high = mixed(a, b, lane)
                s_ref[starts[c] + e, 0:H] = low
                s_ref[starts[c] + e, H:N] = high
                t = t_ref[pl.ds(n * SLAB + within + e, H, stride=8), :]
                moved = pltpu.roll(t, N, axis=1)
                planes.append(low * jnp.where(lane, t, moved))
                planes.append(high * jnp.where(lane, moved, t))
        buffer[0 : 8 * N] = from_right(jnp.concatenate(planes, axis=0), rz[...])

    def rows(n, buffer):
        for e in range(0, 8, 2):
            x = starts[2 * n + e // 4] + e % 4
            a, b = from_left(ly[...], buffer[e * N : (e + 1) * N], buffer[(e + 1) * N : (e + 2) * N])
            one[pl.ds(x * PITCH, N), :] = a
            one[pl.ds((x + 1) * PITCH, N), :] = b
        if after is not None:
            after(n)

    pipelined(depth, rows, count, held)


SHIFTS = ((0, 0), (1, 0), (0, 2), (0, -1), (0, 1), (1, -1), (1, 1), (1, 2))


def chunk_starts():
    tgt = lax.axis_index("tgt")
    z, y, c = tgt // 8, tgt // 2 % 4, tgt % 2
    starts = []
    for dz, dy in SHIFTS:
        for dc in range(2):
            to = ((z + dz) % 2 * 4 + (y + dy + 4) % 4) * 2 + (c + dc) % 2
            starts.append(to * 4)
    return starts


def slab_starts():
    src = lax.axis_index("src")
    x, h = src // 2, src % 2
    starts = []
    for dh in (1, 0):
        for dx in (2, 1, -1, 0):
            starts.append(((x + dx + 4) % 4 * 2 + (h + dh) % 2) * 8)
    return starts


def saved(starts, s_ref, one, s_out, one_out, sems):
    copies = []
    for c, start in enumerate(starts):
        rows = pl.ds(pl.multiple_of(start * PITCH, 8), 4 * PITCH)
        planes = pl.ds(start, 4)
        copies.append(pltpu.make_async_copy(one.at[rows], one_out.at[rows], sems.at[2 * c]))
        copies.append(
            pltpu.make_async_copy(s_ref.at[planes], s_out.at[planes], sems.at[2 * c + 1])
        )
    return copies


def table_plane(y):
    row = lax.broadcasted_iota(jnp.int32, (N, L), 0)
    lane = lax.broadcasted_iota(jnp.int32, (N, L), 1) % N
    x = jnp.where(row > H, row - H, row).astype(jnp.float32)
    z = jnp.where(lane > H, lane - H, lane).astype(jnp.float32)
    return 16.0 / (x * x + z * z + float(y * y) + 0.25)


def early_kernel(*refs):
    chunks, refs = refs[:EARLY], refs[EARLY:]
    t_in, ly, rz, s_out, one_out, k_out, s_ref, one, k_ref, chunk_ref, t_ref, sems, out_sems = refs[:13]
    held = refs[13:]
    starts = chunk_starts()[:EARLY]
    copies = saved(starts, s_ref, one, s_out, one_out, out_sems)
    count = EARLY // 2
    tables = [
        pltpu.make_async_copy(k_ref.at[pl.ds(y, 1)], k_out.at[pl.ds(y, 1)], out_sems.at[2 * EARLY + y])
        for y in range(H + 1)
    ]

    def after(n):
        for copy in copies[4 * n : 4 * n + 4]:
            copy.start()
        for y in range(n * (H + 1) // count, (n + 1) * (H + 1) // count):
            k_ref[y] = table_plane(y)
            tables[y].start()

    refs = (chunk_ref, t_ref, sems, held, ly, rz)
    near_transforms(chunks, starts, t_in, s_ref, one, refs, after)
    for copy in copies + tables:
        copy.wait()


def late_kernel(w_ref, *refs):
    late = 16 - EARLY
    chunks, refs = refs[:late], refs[late:]
    t_in, s_in, one_in, k_in, ly, lx, ix, iy, rz, qz = refs[:10]
    outs, refs = refs[10:18], refs[18:]
    s_ref, one, two, k_ref, chunk_ref, t_ref, near_sems, sems, *held = refs
    starts = chunk_starts()
    copies = saved(starts[:EARLY], s_in, one_in, s_ref, one, sems)
    copies.append(pltpu.make_async_copy(k_in, k_ref, sems.at[2 * EARLY]))
    for copy in copies:
        copy.start()
    refs = (chunk_ref, t_ref, near_sems, held, ly, rz)
    near_transforms(chunks, starts[EARLY:], t_in, s_ref, one, refs)
    for copy in copies:
        copy.wait()

    def planes(n, buffer):
        for e in range(0, BLOCK, 2):
            y = BLOCK * n + e
            a, b = from_left(
                lx[...],
                one[pl.ds(y, N, stride=PITCH), :],
                one[pl.ds(y + 1, N, stride=PITCH), :],
            )
            buffer[e * N : (e + 1) * N] = a * k_ref[y if y <= H else y - H]
            buffer[(e + 1) * N : (e + 2) * N] = b * k_ref[y + 1 if y < H else y + 1 - H]

    def planes_back(n, buffer):
        for e in range(0, BLOCK, 2):
            y = BLOCK * n + e
            a, b = from_left(ix[...], buffer[e * N : (e + 1) * N], buffer[(e + 1) * N : (e + 2) * N])
            two[pl.ds(y * PITCH, N), :] = a
            two[pl.ds((y + 1) * PITCH, N), :] = b

    pipelined(planes, planes_back, N // BLOCK, held)

    lane = lane_mask()
    slabs = slab_starts()
    weight = jnp.where(lax.broadcasted_iota(jnp.int32, (N, L), 1) < N, -w_ref[0], -w_ref[1])

    def rows_back(n, buffer):
        for e in range(0, BLOCK, 2):
            x = slabs[(BLOCK * n + e) // 8] + e % 8
            a, b = from_left(
                iy[...], two[pl.ds(x, N, stride=PITCH), :], two[pl.ds(x + 1, N, stride=PITCH), :]
            )
            buffer[e * N : (e + 1) * N] = a
            buffer[(e + 1) * N : (e + 2) * N] = b

    def depth_back(n, buffer):
        field = from_right(buffer[...], qz[...])
        for e in range(BLOCK):
            slab = (BLOCK * n + e) // 8
            v = field[e * N : (e + 1) * N] * s_ref[slabs[slab] + e % 8] * weight
            low, high = v[:H], v[H:]
            kept = jnp.where(lane, low, high)
            other = jnp.where(lane, high, low)
            outs[slab][pl.ds(e % 8, H, stride=8), :] = kept + pltpu.roll(other, N, axis=1)

    pipelined(rows_back, depth_back, N // BLOCK, held)


def f32(*shape):
    return jax.ShapeDtypeStruct(shape, jnp.float32)


HELD = [pltpu.VMEM((BLOCK * N, L), jnp.float32)] * 2
SMEM = pl.BlockSpec(memory_space=pltpu.SMEM)
ANY = pl.BlockSpec(memory_space=pltpu.HBM)
VMEM = pl.BlockSpec(memory_space=pltpu.VMEM)


def near_scratch(count):
    return [
        pltpu.VMEM((count * CHUNK, L), jnp.float32),
        pltpu.VMEM((count // 2 * SLAB, L), jnp.float32),
        pltpu.SemaphoreType.DMA((3 * count // 2,)),
    ]


def early(chunks, t):
    tables = [jnp.asarray(v) for v in (left_table(BASIS_Y), right_table(BASIS.T))]
    return pl.pallas_call(
        early_kernel,
        in_specs=[ANY] * (EARLY + 1) + [VMEM] * 2,
        out_specs=[ANY] * 3,
        out_shape=(f32(N, N, L), f32(N * PITCH, L), f32(H + 1, N, L)),
        scratch_shapes=[
            pltpu.VMEM((N, N, L), jnp.float32),
            pltpu.VMEM((N * PITCH, L), jnp.float32),
            pltpu.VMEM((H + 1, N, L), jnp.float32),
            *near_scratch(EARLY),
            pltpu.SemaphoreType.DMA((2 * EARLY + H + 1,)),
            *HELD,
        ],
        name="early",
    )(*chunks, t, *tables)


def late(w, chunks, t, s, one, k):
    tables = (
        left_table(BASIS_Y),
        left_table(BASIS),
        left_table(BASIS.T),
        left_table(BASIS_Y.T),
        right_table(BASIS.T),
        right_table(BASIS),
    )
    return pl.pallas_call(
        late_kernel,
        in_specs=[SMEM] + [ANY] * (4 + 16 - EARLY) + [VMEM] * 6,
        out_shape=[f32(SLAB, L)] * 8,
        scratch_shapes=[
            pltpu.VMEM((N, N, L), jnp.float32),
            pltpu.VMEM((N * PITCH, L), jnp.float32),
            pltpu.VMEM((N * PITCH, L), jnp.float32),
            pltpu.VMEM((H + 1, N, L), jnp.float32),
            *near_scratch(16 - EARLY),
            pltpu.SemaphoreType.DMA((2 * EARLY + 1,)),
            *HELD,
        ],
        name="late",
    )(w, *chunks, t, s, one, k, *[jnp.asarray(v) for v in tables])


def tgt_move(value, dz, dy, dc):
    pairs = []
    for z in range(2):
        for y in range(4):
            for c in range(2):
                to = ((z + dz) % 2 * 4 + (y + dy) % 4) * 2 + (c + dc) % 2
                pairs.append(((z * 4 + y) * 2 + c, to))
    return lax.ppermute(value, "tgt", pairs)


def src_move(value, dx, dh):
    pairs = []
    for x in range(4):
        for h in range(2):
            pairs.append((x * 2 + h, (x + dx) % 4 * 2 + (h + dh) % 2))
    return lax.ppermute(value, "src", pairs)


def on_device(targets, sources, occupations):
    own = sources.reshape(2, 4, H, L).transpose(0, 2, 1, 3).reshape(CHUNK, L)
    t = targets.reshape(8, 8, H, L).transpose(0, 2, 1, 3).reshape(8 * SLAB, L)

    across = tgt_move(own, 1, 0, 0)
    far, up, down = (
        tgt_move(own, 0, d, 0) for d in (2, 1, -1)
    )
    sent = [own, across, far, up, down]
    sent += [tgt_move(across, 0, d, 0) for d in (1, -1)]
    sent += [tgt_move(far, 1, 0, 0)]
    other = [tgt_move(v, 0, 0, 1) for v in sent]
    chunks = [v for both in zip(sent, other) for v in both]
    s, one, k = early(chunks[:EARLY], t)
    parts = late(occupations, chunks[EARLY:], t, s, one, k)

    far = src_move(parts[0], 0, 1)
    up = src_move(parts[1], 1, 0)
    down = src_move(parts[2], -1, 0)
    near = [src_move(parts[5], 1, 0), src_move(parts[6], -1, 0)]
    near.append(src_move(parts[4] + far, 2, 0))
    crossed = src_move(parts[3] + up + down, 0, 1)
    total = lax.optimization_barrier(sum(near, parts[7])) + crossed
    return total.reshape(H, 8, L).transpose(1, 0, 2).reshape(1, 8, H * L)


def solution(mesh):
    return jax.shard_map(
        on_device,
        mesh=mesh,
        in_specs=(P("tgt", None, None), P("src", "tgt", None), P("src")),
        out_specs=P("tgt", "src", None),
        check_vma=False,
    )
```

profile of v0, /device:TPU:0, one launch (start us, length us, event | category | flops | bytes accessed | tf_op | source)
XLA Modules:
  0.0 55.4 jit_solution(13213061060056753404)
XLA Ops:
  0.0 2.0 %collective-permute-start = (f32[256,128]{1,0:T(8,128)}, f32[256,128]{1,0:T(8,128)S(1)}, u32[]{:S(2)}, u32[]{:S(2)}) collective-permute-start(f32[256,128]{1,0:T(8,128)} %bitcast.18), channel_id=1, source_target_pairs={{0,64},{8,72},{16,80},{24,88},{32,96},{40,104},{48,112},{56,120},{... | collective-permute-start | bytes 393224 | tf_op jit(solution)/shard_map/ppermute | solution.py:352
  2.0 3.2 %collective-permute-start.5 = (f32[256,128]{1,0:T(8,128)}, f32[256,128]{1,0:T(8,128)S(1)}, u32[]{:S(2)}, u32[]{:S(2)}) collective-permute-start(f32[256,128]{1,0:T(8,128)} %bitcast.19), channel_id=1, source_target_pairs={{0,32},{8,40},{16,48},{24,56},{32,0},{40,8},{48,16},{56,24},{64,96... | collective-permute-start | bytes 393224 | tf_op jit(solution)/shard_map/ppermute | solution.py:352
  5.2 0.7 %collective-permute-start.11 = (f32[256,128]{1,0:T(8,128)}, f32[256,128]{1,0:T(8,128)S(1)}, u32[]{:S(2)}, u32[]{:S(2)}) collective-permute-start(f32[256,128]{1,0:T(8,128)} %bitcast.20), channel_id=1, source_target_pairs={{0,16},{8,24},{16,32},{24,40},{32,48},{40,56},{48,0},{56,8},{64,80... | collective-permute-start | bytes 393224 | tf_op jit(solution)/shard_map/ppermute | solution.py:352
  5.9 2.6 %collective-permute-start.13 = (f32[256,128]{1,0:T(8,128)}, f32[256,128]{1,0:T(8,128)S(1)}, u32[]{:S(2)}, u32[]{:S(2)}) collective-permute-start(f32[256,128]{1,0:T(8,128)} %bitcast.21), channel_id=1, source_target_pairs={{0,48},{8,56},{16,0},{24,8},{32,16},{40,24},{48,32},{56,40},{64,11... | collective-permute-start | bytes 393224 | tf_op jit(solution)/shard_map/ppermute | solution.py:352
  9.0 0.7 %collective-permute-done.5.refs_4_ = f32[256,128]{1,0:T(8,128)S(1)} collective-permute-done((f32[256,128]{1,0:T(8,128)}, f32[256,128]{1,0:T(8,128)S(1)}, u32[]{:S(2)}, u32[]{:S(2)}) %collective-permute-start.5) | collective-permute-done | bytes 131104 | tf_op jit(solution)/shard_map/ppermute | solution.py:352
  9.7 2.2 %collective-permute-done.11.refs_6_ = f32[256,128]{1,0:T(8,128)S(1)} collective-permute-done((f32[256,128]{1,0:T(8,128)}, f32[256,128]{1,0:T(8,128)S(1)}, u32[]{:S(2)}, u32[]{:S(2)}) %collective-permute-start.11) | collective-permute-done | bytes 131104 | tf_op jit(solution)/shard_map/ppermute | solution.py:352
  11.9 1.4 %collective-permute-start.1 = (f32[256,128]{1,0:T(8,128)S(1)}, f32[256,128]{1,0:T(8,128)S(1)}, u32[]{:S(2)}, u32[]{:S(2)}) collective-permute-start(f32[256,128]{1,0:T(8,128)S(1)} %collective-permute-done.refs_2_), channel_id=1, source_target_pairs={{0,16},{8,24},{16,32},{24,40},{32,48},{40,56},{48,0},{56,8},{64,80... | collective-permute-start | bytes 393224 | tf_op jit(solution)/shard_map/ppermute | solution.py:352
  13.3 1.9 %collective-permute-start.3 = (f32[256,128]{1,0:T(8,128)S(1)}, f32[256,128]{1,0:T(8,128)S(1)}, u32[]{:S(2)}, u32[]{:S(2)}) collective-permute-start(f32[256,128]{1,0:T(8,128)S(1)} %collective-permute-done.refs_2_), channel_id=1, source_target_pairs={{0,48},{8,56},{16,0},{24,8},{32,16},{40,24},{48,32},{56,40},{64,11... | collective-permute-start | bytes 393224 | tf_op jit(solution)/shard_map/ppermute | solution.py:352
  15.9 2.1 %collective-permute-done.1.refs_0_ = f32[256,128]{1,0:T(8,128)S(1)} collective-permute-done((f32[256,128]{1,0:T(8,128)S(1)}, f32[256,128]{1,0:T(8,128)S(1)}, u32[]{:S(2)}, u32[]{:S(2)}) %collective-permute-start.1) | collective-permute-done | bytes 131104 | tf_op jit(solution)/shard_map/ppermute | solution.py:352
  18.6 1.5 %collective-permute-done.6.refs_4_ = f32[256,128]{1,0:T(8,128)S(1)} collective-permute-done((f32[256,128]{1,0:T(8,128)S(1)}, f32[256,128]{1,0:T(8,128)S(1)}, u32[]{:S(2)}, u32[]{:S(2)}) %collective-permute-start.6) | collective-permute-done | bytes 131104 | tf_op jit(solution)/shard_map/ppermute | solution.py:352
  20.9 5.5 %early.1 = (f32[64,64,128]{2,1,0:T(8,128)}, f32[4224,128]{1,0:T(8,128)}, f32[33,64,128]{2,1,0:T(8,128)}) custom-call(f32[256,128]{1,0:T(8,128)} %bitcast.23, f32[256,128]{1,0:T(8,128)} %copy-done.10, f32[256,128]{1,0:T(8,128)} %copy-done.6, f32[256,128]{1,0:T(8,128)} %copy-done.11, f32[256,128]{1,0:T(8,128)} %copy-done.7, f32[256,128]{1,0:T(8,128)} %copy-done.12, ...), custom_call_target="tpu_custom_call" | custom-call | tf_op jit(solution)/shard_map/early/pallas_call | solution.py:302
  27.2 8.0 %late.1 = (f32[256,128]{1,0:T(8,128)}, f32[256,128]{1,0:T(8,128)}, f32[256,128]{1,0:T(8,128)}, f32[256,128]{1,0:T(8,128)}, f32[256,128]{1,0:T(8,128)}, /*index=5...) custom-call(f32[2]{0:T(128)} %w_ref.1, f32[256,128]{1,0:T(8,128)} %copy-done, f32[256,128]{1,0:T(8,128)} %copy-done.3, ...), custom_call_target="tpu_custom_call" | custom-call | tf_op jit(solution)/shard_map/late/pallas_call | solution.py:328
  35.2 3.6 %collective-permute-start.17 = (f32[256,128]{1,0:T(8,128)}, f32[256,128]{1,0:T(8,128)S(1)}, u32[]{:S(2)}, u32[]{:S(2)}) collective-permute-start(f32[256,128]{1,0:T(8,128)} %get-tuple-element.23), channel_id=1, source_target_pairs={{0,1},{1,0},{2,3},{3,2},{4,5},{5,4},{6,7},{7,6},{8,9},{9,8},{10,11... | collective-permute-start | bytes 393224 | tf_op jit(solution)/shard_map/ppermute | solution.py:360
  38.9 1.5 %collective-permute-start.19 = (f32[256,128]{1,0:T(8,128)}, f32[256,128]{1,0:T(8,128)S(1)}, u32[]{:S(2)}, u32[]{:S(2)}) collective-permute-start(f32[256,128]{1,0:T(8,128)} %get-tuple-element.25), channel_id=1, source_target_pairs={{0,2},{1,3},{2,4},{3,5},{4,6},{5,7},{6,0},{7,1},{8,10},{9,11},{10,... | collective-permute-start | bytes 393224 | tf_op jit(solution)/shard_map/ppermute | solution.py:360
  40.3 1.8 %collective-permute-start.20 = (f32[256,128]{1,0:T(8,128)}, f32[256,128]{1,0:T(8,128)S(1)}, u32[]{:S(2)}, u32[]{:S(2)}) collective-permute-start(f32[256,128]{1,0:T(8,128)} %get-tuple-element.26), channel_id=1, source_target_pairs={{0,6},{1,7},{2,0},{3,1},{4,2},{5,3},{6,4},{7,5},{8,14},{9,15},{10,... | collective-permute-start | bytes 393224 | tf_op jit(solution)/shard_map/ppermute | solution.py:360
  42.4 3.0 %collective-permute-start.16 = (f32[256,128]{1,0:T(8,128)}, f32[256,128]{1,0:T(8,128)S(1)}, u32[]{:S(2)}, u32[]{:S(2)}) collective-permute-start(f32[256,128]{1,0:T(8,128)} %get-tuple-element.21), channel_id=1, source_target_pairs={{0,6},{1,7},{2,0},{3,1},{4,2},{5,3},{6,4},{7,5},{8,14},{9,15},{10,... | collective-permute-start | bytes 393224 | tf_op jit(solution)/shard_map/ppermute | solution.py:360
  45.3 0.9 %add.23 = f32[256,128]{1,0:T(8,128)S(1)} add(f32[256,128]{1,0:T(8,128)} %get-tuple-element.22, f32[256,128]{1,0:T(8,128)S(1)} %collective-permute-done.17) | non-fusion elementwise | flops 32768 | bytes 393216 | tf_op jit(solution)/shard_map/add | solution.py:383
  46.3 1.0 %collective-permute-start.18 = (f32[256,128]{1,0:T(8,128)S(1)}, f32[256,128]{1,0:T(8,128)S(1)}, u32[]{:S(2)}, u32[]{:S(2)}) collective-permute-start(f32[256,128]{1,0:T(8,128)S(1)} %add.23), channel_id=1, source_target_pairs={{0,4},{1,5},{2,6},{3,7},{4,0},{5,1},{6,2},{7,3},{8,12},{9,13},{10,... | collective-permute-start | bytes 393224 | tf_op jit(solution)/shard_map/ppermute | solution.py:360
  47.2 0.9 %add_add_fusion = f32[256,128]{1,0:T(8,128)S(1)} fusion(f32[256,128]{1,0:T(8,128)S(1)} %collective-permute-done.20, f32[256,128]{1,0:T(8,128)} %get-tuple-element.24, f32[256,128]{1,0:T(8,128)S(1)} %collective-permute-done.19), kind=kLoop, calls=%fused_computation.1 | loop fusion | flops 65536 | bytes 524288 | tf_op jit(solution)/shard_map/add | solution.py:384
  48.2 3.3 %collective-permute-start.21 = (f32[256,128]{1,0:T(8,128)S(1)}, f32[256,128]{1,0:T(8,128)S(1)}, u32[]{:S(2)}, u32[]{:S(2)}) collective-permute-start(f32[256,128]{1,0:T(8,128)S(1)} %add_add_fusion), channel_id=1, source_target_pairs={{0,1},{1,0},{2,3},{3,2},{4,5},{5,4},{6,7},{7,6},{8,9},{9,8},{10,11... | collective-permute-start | bytes 393224 | tf_op jit(solution)/shard_map/ppermute | solution.py:360
  51.5 1.3 %collective-permute-done.18 = f32[256,128]{1,0:T(8,128)S(1)} collective-permute-done((f32[256,128]{1,0:T(8,128)S(1)}, f32[256,128]{1,0:T(8,128)S(1)}, u32[]{:S(2)}, u32[]{:S(2)}) %collective-permute-start.18) | collective-permute-done | bytes 131104 | tf_op jit(solution)/shard_map/ppermute | solution.py:360
  52.8 0.9 %add_add_fusion.1 = f32[256,128]{1,0:T(8,128)S(1)} fusion(f32[256,128]{1,0:T(8,128)S(1)} %collective-permute-done.18, f32[256,128]{1,0:T(8,128)S(1)} %collective-permute-done.16, f32[256,128]{1,0:T(8,128)} %get-tuple-element.19, f32[256,128]{1,0:T(8,128)S(1)} %collective-permute-done.15), kind=kLoop, calls=%fused_computation.2 | loop fusion | flops 98304 | bytes 655360 | tf_op jit(solution)/shard_map/add | solution.py:385
  53.8 1.0 %collective-permute-done.21 = f32[256,128]{1,0:T(8,128)S(1)} collective-permute-done((f32[256,128]{1,0:T(8,128)S(1)}, f32[256,128]{1,0:T(8,128)S(1)}, u32[]{:S(2)}, u32[]{:S(2)}) %collective-permute-start.21) | collective-permute-done | bytes 131104 | tf_op jit(solution)/shard_map/ppermute | solution.py:360
  54.7 0.7 %add_bitcast_fusion = f32[1,8,4096]{2,1,0:T(8,128)} fusion(f32[256,128]{1,0:T(8,128)S(1)} %add_add_fusion.1, f32[256,128]{1,0:T(8,128)S(1)} %collective-permute-done.21), kind=kLoop, calls=%fused_computation | loop fusion | flops 32768 | bytes 393216 | tf_op jit(solution)/shard_map/reshape | solution.py:386
  (56 shorter events, 3.5 us)
Async XLA Ops:
  0.0 8.5 %collective-permute-start = (f32[256,128]{1,0:T(8,128)}, f32[256,128]{1,0:T(8,128)S(1)}, u32[]{:S(2)}, u32[]{:S(2)}) collective-permute-start(f32[256,128]{1,0:T(8,128)} %bitcast.18), channel_id=1, source_target_pairs={{0,64},{8,72},{16,80},{24,88},{32,96},{40,104},{48,112},{56,120},{... | collective-permute-start | bytes 393224 | tf_op jit(solution)/shard_map/ppermute | solution.py:352
  2.0 7.6 %collective-permute-start.5 = (f32[256,128]{1,0:T(8,128)}, f32[256,128]{1,0:T(8,128)S(1)}, u32[]{:S(2)}, u32[]{:S(2)}) collective-permute-start(f32[256,128]{1,0:T(8,128)} %bitcast.19), channel_id=1, source_target_pairs={{0,32},{8,40},{16,48},{24,56},{32,0},{40,8},{48,16},{56,24},{64,96... | collective-permute-start | bytes 393224 | tf_op jit(solution)/shard_map/ppermute | solution.py:352
  5.2 6.7 %collective-permute-start.11 = (f32[256,128]{1,0:T(8,128)}, f32[256,128]{1,0:T(8,128)S(1)}, u32[]{:S(2)}, u32[]{:S(2)}) collective-permute-start(f32[256,128]{1,0:T(8,128)} %bitcast.20), channel_id=1, source_target_pairs={{0,16},{8,24},{16,32},{24,40},{32,48},{40,56},{48,0},{56,8},{64,80... | collective-permute-start | bytes 393224 | tf_op jit(solution)/shard_map/ppermute | solution.py:352
  5.9 7.3 %collective-permute-start.13 = (f32[256,128]{1,0:T(8,128)}, f32[256,128]{1,0:T(8,128)S(1)}, u32[]{:S(2)}, u32[]{:S(2)}) collective-permute-start(f32[256,128]{1,0:T(8,128)} %bitcast.21), channel_id=1, source_target_pairs={{0,48},{8,56},{16,0},{24,8},{32,16},{40,24},{48,32},{56,40},{64,11... | collective-permute-start | bytes 393224 | tf_op jit(solution)/shard_map/ppermute | solution.py:352
  8.5 6.7 %collective-permute-start.8 = (f32[256,128]{1,0:T(8,128)}, f32[256,128]{1,0:T(8,128)S(1)}, u32[]{:S(2)}, u32[]{:S(2)}) collective-permute-start(f32[256,128]{1,0:T(8,128)} %bitcast.22), channel_id=1, source_target_pairs={{0,8},{8,0},{16,24},{24,16},{32,40},{40,32},{48,56},{56,48},{64,72... | collective-permute-start | bytes 393224 | tf_op jit(solution)/shard_map/ppermute | solution.py:352
  8.5 11.7 %copy-start.6 = (f32[256,128]{1,0:T(8,128)}, f32[256,128]{1,0:T(8,128)S(1)}, u32[]{:S(2)}) copy-start(f32[256,128]{1,0:T(8,128)S(1)} %collective-permute-done.refs_2_) | copy-start | bytes 393220
  8.5 7.0 %collective-permute-start.9 = (f32[256,128]{1,0:T(8,128)S(1)}, f32[256,128]{1,0:T(8,128)S(1)}, u32[]{:S(2)}, u32[]{:S(2)}) collective-permute-start(f32[256,128]{1,0:T(8,128)S(1)} %collective-permute-done.refs_2_), channel_id=1, source_target_pairs={{0,8},{8,0},{16,24},{24,16},{32,40},{40,32},{48,56},{56,48},{64,72... | collective-permute-start | bytes 393224 | tf_op jit(solution)/shard_map/ppermute | solution.py:352
  9.6 10.5 %copy-start.7 = (f32[256,128]{1,0:T(8,128)}, f32[256,128]{1,0:T(8,128)S(1)}, u32[]{:S(2)}) copy-start(f32[256,128]{1,0:T(8,128)S(1)} %collective-permute-done.5.refs_4_) | copy-start | bytes 393220
  9.6 5.8 %collective-permute-start.10 = (f32[256,128]{1,0:T(8,128)S(1)}, f32[256,128]{1,0:T(8,128)S(1)}, u32[]{:S(2)}, u32[]{:S(2)}) collective-permute-start(f32[256,128]{1,0:T(8,128)S(1)} %collective-permute-done.5.refs_4_), channel_id=1, source_target_pairs={{0,8},{8,0},{16,24},{24,16},{32,40},{40,32},{48,56},{56,48},{64,72... | collective-permute-start | bytes 393224 | tf_op jit(solution)/shard_map/ppermute | solution.py:352
  11.9 6.2 %collective-permute-start.1 = (f32[256,128]{1,0:T(8,128)S(1)}, f32[256,128]{1,0:T(8,128)S(1)}, u32[]{:S(2)}, u32[]{:S(2)}) collective-permute-start(f32[256,128]{1,0:T(8,128)S(1)} %collective-permute-done.refs_2_), channel_id=1, source_target_pairs={{0,16},{8,24},{16,32},{24,40},{32,48},{40,56},{48,0},{56,8},{64,80... | collective-permute-start | bytes 393224 | tf_op jit(solution)/shard_map/ppermute | solution.py:352
  13.3 5.0 %collective-permute-start.3 = (f32[256,128]{1,0:T(8,128)S(1)}, f32[256,128]{1,0:T(8,128)S(1)}, u32[]{:S(2)}, u32[]{:S(2)}) collective-permute-start(f32[256,128]{1,0:T(8,128)S(1)} %collective-permute-done.refs_2_), channel_id=1, source_target_pairs={{0,48},{8,56},{16,0},{24,8},{32,16},{40,24},{48,32},{56,40},{64,11... | collective-permute-start | bytes 393224 | tf_op jit(solution)/shard_map/ppermute | solution.py:352
  15.1 5.0 %collective-permute-start.6 = (f32[256,128]{1,0:T(8,128)S(1)}, f32[256,128]{1,0:T(8,128)S(1)}, u32[]{:S(2)}, u32[]{:S(2)}) collective-permute-start(f32[256,128]{1,0:T(8,128)S(1)} %collective-permute-done.5.refs_4_), channel_id=1, source_target_pairs={{0,64},{8,72},{16,80},{24,88},{32,96},{40,104},{48,112},{56,120},{... | collective-permute-start | bytes 393224 | tf_op jit(solution)/shard_map/ppermute | solution.py:352
  15.4 4.7 %collective-permute-start.12 = (f32[256,128]{1,0:T(8,128)S(1)}, f32[256,128]{1,0:T(8,128)S(1)}, u32[]{:S(2)}, u32[]{:S(2)}) collective-permute-start(f32[256,128]{1,0:T(8,128)S(1)} %collective-permute-done.11.refs_6_), channel_id=1, source_target_pairs={{0,8},{8,0},{16,24},{24,16},{32,40},{40,32},{48,56},{56,48},{64,72... | collective-permute-start | bytes 393224 | tf_op jit(solution)/shard_map/ppermute | solution.py:352
  15.5 4.7 %collective-permute-start.14 = (f32[256,128]{1,0:T(8,128)S(1)}, f32[256,128]{1,0:T(8,128)S(1)}, u32[]{:S(2)}, u32[]{:S(2)}) collective-permute-start(f32[256,128]{1,0:T(8,128)S(1)} %collective-permute-done.13.refs_8_), channel_id=1, source_target_pairs={{0,8},{8,0},{16,24},{24,16},{32,40},{40,32},{48,56},{56,48},{64,72... | collective-permute-start | bytes 393224 | tf_op jit(solution)/shard_map/ppermute | solution.py:352
  18.1 8.3 %collective-permute-start.2 = (f32[256,128]{1,0:T(8,128)S(1)}, f32[256,128]{1,0:T(8,128)S(1)}, u32[]{:S(2)}, u32[]{:S(2)}) collective-permute-start(f32[256,128]{1,0:T(8,128)S(1)} %collective-permute-done.1.refs_0_), channel_id=1, source_target_pairs={{0,8},{8,0},{16,24},{24,16},{32,40},{40,32},{48,56},{56,48},{64,72... | collective-permute-start | bytes 393224 | tf_op jit(solution)/shard_map/ppermute | solution.py:352
  18.2 8.2 %collective-permute-start.4 = (f32[256,128]{1,0:T(8,128)S(1)}, f32[256,128]{1,0:T(8,128)S(1)}, u32[]{:S(2)}, u32[]{:S(2)}) collective-permute-start(f32[256,128]{1,0:T(8,128)S(1)} %collective-permute-done.3.refs_2_), channel_id=1, source_target_pairs={{0,8},{8,0},{16,24},{24,16},{32,40},{40,32},{48,56},{56,48},{64,72... | collective-permute-start | bytes 393224 | tf_op jit(solution)/shard_map/ppermute | solution.py:352
  20.1 6.3 %collective-permute-start.7 = (f32[256,128]{1,0:T(8,128)S(1)}, f32[256,128]{1,0:T(8,128)S(1)}, u32[]{:S(2)}, u32[]{:S(2)}) collective-permute-start(f32[256,128]{1,0:T(8,128)S(1)} %collective-permute-done.6.refs_4_), channel_id=1, source_target_pairs={{0,8},{8,0},{16,24},{24,16},{32,40},{40,32},{48,56},{56,48},{64,72... | collective-permute-start | bytes 393224 | tf_op jit(solution)/shard_map/ppermute | solution.py:352
  35.2 10.1 %collective-permute-start.17 = (f32[256,128]{1,0:T(8,128)}, f32[256,128]{1,0:T(8,128)S(1)}, u32[]{:S(2)}, u32[]{:S(2)}) collective-permute-start(f32[256,128]{1,0:T(8,128)} %get-tuple-element.23), channel_id=1, source_target_pairs={{0,1},{1,0},{2,3},{3,2},{4,5},{5,4},{6,7},{7,6},{8,9},{9,8},{10,11... | collective-permute-start | bytes 393224 | tf_op jit(solution)/shard_map/ppermute | solution.py:360
  38.9 8.4 %collective-permute-start.19 = (f32[256,128]{1,0:T(8,128)}, f32[256,128]{1,0:T(8,128)S(1)}, u32[]{:S(2)}, u32[]{:S(2)}) collective-permute-start(f32[256,128]{1,0:T(8,128)} %get-tuple-element.25), channel_id=1, source_target_pairs={{0,2},{1,3},{2,4},{3,5},{4,6},{5,7},{6,0},{7,1},{8,10},{9,11},{10,... | collective-permute-start | bytes 393224 | tf_op jit(solution)/shard_map/ppermute | solution.py:360
  40.3 6.9 %collective-permute-start.20 = (f32[256,128]{1,0:T(8,128)}, f32[256,128]{1,0:T(8,128)S(1)}, u32[]{:S(2)}, u32[]{:S(2)}) collective-permute-start(f32[256,128]{1,0:T(8,128)} %get-tuple-element.26), channel_id=1, source_target_pairs={{0,6},{1,7},{2,0},{3,1},{4,2},{5,3},{6,4},{7,5},{8,14},{9,15},{10,... | collective-permute-start | bytes 393224 | tf_op jit(solution)/shard_map/ppermute | solution.py:360
  42.1 9.4 %collective-permute-start.15 = (f32[256,128]{1,0:T(8,128)}, f32[256,128]{1,0:T(8,128)S(1)}, u32[]{:S(2)}, u32[]{:S(2)}) collective-permute-start(f32[256,128]{1,0:T(8,128)} %get-tuple-element.20), channel_id=1, source_target_pairs={{0,2},{1,3},{2,4},{3,5},{4,6},{5,7},{6,0},{7,1},{8,10},{9,11},{10,... | collective-permute-start | bytes 393224 | tf_op jit(solution)/shard_map/ppermute | solution.py:360
  42.4 9.1 %collective-permute-start.16 = (f32[256,128]{1,0:T(8,128)}, f32[256,128]{1,0:T(8,128)S(1)}, u32[]{:S(2)}, u32[]{:S(2)}) collective-permute-start(f32[256,128]{1,0:T(8,128)} %get-tuple-element.21), channel_id=1, source_target_pairs={{0,6},{1,7},{2,0},{3,1},{4,2},{5,3},{6,4},{7,5},{8,14},{9,15},{10,... | collective-permute-start | bytes 393224 | tf_op jit(solution)/shard_map/ppermute | solution.py:360
  46.3 6.6 %collective-permute-start.18 = (f32[256,128]{1,0:T(8,128)S(1)}, f32[256,128]{1,0:T(8,128)S(1)}, u32[]{:S(2)}, u32[]{:S(2)}) collective-permute-start(f32[256,128]{1,0:T(8,128)S(1)} %add.23), channel_id=1, source_target_pairs={{0,4},{1,5},{2,6},{3,7},{4,0},{5,1},{6,2},{7,3},{8,12},{9,13},{10,... | collective-permute-start | bytes 393224 | tf_op jit(solution)/shard_map/ppermute | solution.py:360
  48.2 6.6 %collective-permute-start.21 = (f32[256,128]{1,0:T(8,128)S(1)}, f32[256,128]{1,0:T(8,128)S(1)}, u32[]{:S(2)}, u32[]{:S(2)}) collective-permute-start(f32[256,128]{1,0:T(8,128)S(1)} %add_add_fusion), channel_id=1, source_target_pairs={{0,1},{1,0},{2,3},{3,2},{4,5},{5,4},{6,7},{7,6},{8,9},{9,8},{10,11... | collective-permute-start | bytes 393224 | tf_op jit(solution)/shard_map/ppermute | solution.py:360
  (13 other events, 56.4 us)
where the time goes:
time: 55.6 us; the launch traced here: 55.4 us
  starting transfers between devices  27.7 us (50%)
  Pallas kernels  13.5 us (24%)
  waiting for transfers between devices  9.04 us (16%)
  other arithmetic  3.47 us (6%)
  local copies, waits for them, and re-layouts  1.4 us (3%)
    ppermute x7, starting transfers between devices, src_move(): return lax.ppermute(value, 'src', pairs)  14.4 us
    ppermute x15, starting transfers between devices, tgt_move(): return lax.ppermute(value, 'tgt', pairs)  13.4 us
    pallas_call x1, Pallas kernels, late(): pl.pallas_call(late_kernel, in_specs=[SMEM] + [ANY] * (4 + 16 - EARLY) +...  8.02 us
    ppermute x15, waiting for transfers between devices, tgt_move(): return lax.ppermute(value, 'tgt', pairs)  6.72 us
    pallas_call x1, Pallas kernels, early(): pl.pallas_call(early_kernel, in_specs=[ANY] * (EARLY + 1) + [VMEM] * 2, o...  5.51 us
    ppermute x7, waiting for transfers between devices, src_move(): return lax.ppermute(value, 'src', pairs)  2.32 us
    unnamed x30, local copies, waits for them, and re-layouts  1.4 us
  transfers between devices with their start and end apart: 22, of which 7 were waited for; matrix products, arithmetic and copies ran while one was open for 5% of the time, Pallas kernels for 10%

commit v1 on v0

--- a/solution.py
+++ b/solution.py
@@ -13,7 +13,6 @@
 BLOCK = 16
 CHUNK = 2 * H * 4
 SLAB = H * 8
-EARLY = 10
 
 
 def real_basis():
@@ -97,43 +96,21 @@
     return low, high
 
 
-def near_transforms(chunks, starts, t_in, s_ref, one, refs, after=None):
-    chunk_ref, t_ref, sems, held, ly, rz = refs
+def near_transforms(chunks, starts, t_ref, s_ref, one, held, ly, rz):
     lane = lane_mask()
-    count = len(starts) // 2
-    copies = []
-    for n in range(count):
-        group = pl.ds(pl.multiple_of(starts[2 * n] // 8 * SLAB, SLAB), SLAB)
-        wanted = [
-            pltpu.make_async_copy(t_in.at[group], t_ref.at[pl.ds(n * SLAB, SLAB)], sems.at[3 * n])
-        ]
-        for e in range(2):
-            c = 2 * n + e
-            wanted.append(
-                pltpu.make_async_copy(
-                    chunks[c], chunk_ref.at[pl.ds(c * CHUNK, CHUNK)], sems.at[3 * n + 1 + e]
-                )
-            )
-        for copy in wanted:
-            copy.start()
-        copies.append(wanted)
 
     def depth(n, buffer):
-        for copy in copies[n]:
-            copy.wait()
         planes = []
         for c in range(2 * n, 2 * n + 2):
-            within = starts[c] % 8
             for e in range(4):
-                a = chunk_ref[pl.ds(c * CHUNK + e, H, stride=4), :]
-                b = chunk_ref[pl.ds(c * CHUNK + CHUNK // 2 + e, H, stride=4), :]
+                a = chunks[c][pl.ds(e, H, stride=4), :]
+                b = chunks[c][pl.ds(CHUNK // 2 + e, H, stride=4), :]
                 low, high = mixed(a, b, lane)
-                s_ref[starts[c] + e, 0:H] = low
-                s_ref[starts[c] + e, H:N] = high
-                t = t_ref[pl.ds(n * SLAB + within + e, H, stride=8), :]
-                moved = pltpu.roll(t, N, axis=1)
-                planes.append(low * jnp.where(lane, t, moved))
-                planes.append(high * jnp.where(lane, moved, t))
+                x = starts[c] + e
+                s_ref[x, 0:H] = low
+                s_ref[x, H:N] = high
+                planes.append(low * t_ref[x, 0:H])
+                planes.append(high * t_ref[x, H:N])
         buffer[0 : 8 * N] = from_right(jnp.concatenate(planes, axis=0), rz[...])
 
     def rows(n, buffer):
@@ -142,10 +119,8 @@
             a, b = from_left(ly[...], buffer[e * N : (e + 1) * N], buffer[(e + 1) * N : (e + 2) * N])
             one[pl.ds(x * PITCH, N), :] = a
             one[pl.ds((x + 1) * PITCH, N), :] = b
-        if after is not None:
-            after(n)
-
-    pipelined(depth, rows, count, held)
+
+    pipelined(depth, rows, len(starts) // 2, held)
 
 
 SHIFTS = ((0, 0), (1, 0), (0, 2), (0, -1), (0, 1), (1, -1), (1, 1), (1, 2))
@@ -172,66 +147,46 @@
     return starts
 
 
-def saved(starts, s_ref, one, s_out, one_out, sems):
-    copies = []
-    for c, start in enumerate(starts):
-        rows = pl.ds(pl.multiple_of(start * PITCH, 8), 4 * PITCH)
-        planes = pl.ds(start, 4)
-        copies.append(pltpu.make_async_copy(one.at[rows], one_out.at[rows], sems.at[2 * c]))
-        copies.append(
-            pltpu.make_async_copy(s_ref.at[planes], s_out.at[planes], sems.at[2 * c + 1])
-        )
-    return copies
-
-
-def table_plane(y):
-    row = lax.broadcasted_iota(jnp.int32, (N, L), 0)
-    lane = lax.broadcasted_iota(jnp.int32, (N, L), 1) % N
-    x = jnp.where(row > H, row - H, row).astype(jnp.float32)
-    z = jnp.where(lane > H, lane - H, lane).astype(jnp.float32)
-    return 16.0 / (x * x + z * z + float(y * y) + 0.25)
-
-
-def early_kernel(*refs):
-    chunks, refs = refs[:EARLY], refs[EARLY:]
-    t_in, ly, rz, s_out, one_out, k_out, s_ref, one, k_ref, chunk_ref, t_ref, sems, out_sems = refs[:13]
-    held = refs[13:]
-    starts = chunk_starts()[:EARLY]
-    copies = saved(starts, s_ref, one, s_out, one_out, out_sems)
-    count = EARLY // 2
-    tables = [
-        pltpu.make_async_copy(k_ref.at[pl.ds(y, 1)], k_out.at[pl.ds(y, 1)], out_sems.at[2 * EARLY + y])
-        for y in range(H + 1)
-    ]
-
-    def after(n):
-        for copy in copies[4 * n : 4 * n + 4]:
-            copy.start()
-        for y in range(n * (H + 1) // count, (n + 1) * (H + 1) // count):
-            k_ref[y] = table_plane(y)
-            tables[y].start()
-
-    refs = (chunk_ref, t_ref, sems, held, ly, rz)
-    near_transforms(chunks, starts, t_in, s_ref, one, refs, after)
-    for copy in copies + tables:
-        copy.wait()
-
-
-def late_kernel(w_ref, *refs):
-    late = 16 - EARLY
-    chunks, refs = refs[:late], refs[late:]
-    t_in, s_in, one_in, k_in, ly, lx, ix, iy, rz, qz = refs[:10]
-    outs, refs = refs[10:18], refs[18:]
-    s_ref, one, two, k_ref, chunk_ref, t_ref, near_sems, sems, *held = refs
-    starts = chunk_starts()
-    copies = saved(starts[:EARLY], s_in, one_in, s_ref, one, sems)
-    copies.append(pltpu.make_async_copy(k_in, k_ref, sems.at[2 * EARLY]))
+def prepare_kernel(w_ref, raw, *refs):
+    tables, (w_out, t_ref, k_ref, *outs), (t_in, sems) = refs[:7], refs[7:17], refs[17:]
+    copies = [pltpu.make_async_copy(raw, t_in, sems.at[7])]
+    for n, (table, out) in enumerate(zip(tables, outs)):
+        copies.append(pltpu.make_async_copy(table, out, sems.at[n]))
     for copy in copies:
         copy.start()
-    refs = (chunk_ref, t_ref, near_sems, held, ly, rz)
-    near_transforms(chunks, starts[EARLY:], t_in, s_ref, one, refs)
+    half = lax.broadcasted_iota(jnp.int32, (8, L), 1) < N
+    w_out[...] = jnp.where(half, -w_ref[0], -w_ref[1])
+    lane = lane_mask()
+
+    row = lax.broadcasted_iota(jnp.int32, (N, L), 0)
+    column = lax.broadcasted_iota(jnp.int32, (N, L), 1) % N
+    x = jnp.where(row > H, row - H, row).astype(jnp.float32)
+    z = jnp.where(column > H, column - H, column).astype(jnp.float32)
+    base = x * x + z * z + 0.25
+
+    def body(y, _):
+        k_ref[y] = 16.0 / (base + (y * y).astype(jnp.float32))
+        return 0
+
+    lax.fori_loop(0, H + 1, body, 0, unroll=3)
     for copy in copies:
         copy.wait()
+
+    def target(x, _):
+        t = t_in[pl.ds(x // 8 * SLAB + x % 8, H, stride=8), :]
+        moved = pltpu.roll(t, N, axis=1)
+        t_ref[x, 0:H] = jnp.where(lane, t, moved)
+        t_ref[x, H:N] = jnp.where(lane, moved, t)
+        return 0
+
+    lax.fori_loop(0, N, target, 0, unroll=8)
+
+
+def late_kernel(*refs):
+    chunks, refs = refs[:16], refs[16:]
+    w_ref, t_ref, k_ref, ly, lx, ix, iy, rz, qz = refs[:9]
+    outs, (s_ref, one, two, *held) = refs[9:17], refs[17:]
+    near_transforms(chunks, chunk_starts(), t_ref, s_ref, one, held, ly, rz)
 
     def planes(n, buffer):
         for e in range(0, BLOCK, 2):
@@ -255,7 +210,7 @@
 
     lane = lane_mask()
     slabs = slab_starts()
-    weight = jnp.where(lax.broadcasted_iota(jnp.int32, (N, L), 1) < N, -w_ref[0], -w_ref[1])
+    weight = w_ref[0:1]
 
     def rows_back(n, buffer):
         for e in range(0, BLOCK, 2):
@@ -279,44 +234,21 @@
     pipelined(rows_back, depth_back, N // BLOCK, held)
 
 
-def f32(*shape):
-    return jax.ShapeDtypeStruct(shape, jnp.float32)
-
-
 HELD = [pltpu.VMEM((BLOCK * N, L), jnp.float32)] * 2
 SMEM = pl.BlockSpec(memory_space=pltpu.SMEM)
 ANY = pl.BlockSpec(memory_space=pltpu.HBM)
 VMEM = pl.BlockSpec(memory_space=pltpu.VMEM)
 
 
-def near_scratch(count):
-    return [
-        pltpu.VMEM((count * CHUNK, L), jnp.float32),
-        pltpu.VMEM((count // 2 * SLAB, L), jnp.float32),
-        pltpu.SemaphoreType.DMA((3 * count // 2,)),
-    ]
-
-
-def early(chunks, t):
-    tables = [jnp.asarray(v) for v in (left_table(BASIS_Y), right_table(BASIS.T))]
-    return pl.pallas_call(
-        early_kernel,
-        in_specs=[ANY] * (EARLY + 1) + [VMEM] * 2,
-        out_specs=[ANY] * 3,
-        out_shape=(f32(N, N, L), f32(N * PITCH, L), f32(H + 1, N, L)),
-        scratch_shapes=[
-            pltpu.VMEM((N, N, L), jnp.float32),
-            pltpu.VMEM((N * PITCH, L), jnp.float32),
-            pltpu.VMEM((H + 1, N, L), jnp.float32),
-            *near_scratch(EARLY),
-            pltpu.SemaphoreType.DMA((2 * EARLY + H + 1,)),
-            *HELD,
-        ],
-        name="early",
-    )(*chunks, t, *tables)
-
-
-def late(w, chunks, t, s, one, k):
+def far_off(value):
+    return pltpu.with_memory_space_constraint(value, pltpu.HBM)
+
+
+def near(value):
+    return pltpu.with_memory_space_constraint(value, pltpu.VMEM)
+
+
+def prepare(w, t, own):
     tables = (
         left_table(BASIS_Y),
         left_table(BASIS),
@@ -325,21 +257,34 @@
         right_table(BASIS.T),
         right_table(BASIS),
     )
+    shapes = [((8, L), jnp.float32), ((N, N, L), jnp.float32), ((H + 1, N, L), jnp.float32)]
+    shapes += [((CHUNK, L), jnp.float32)] + [(v.shape, jnp.bfloat16) for v in tables]
+    return pl.pallas_call(
+        prepare_kernel,
+        in_specs=[SMEM] + [ANY] * 8,
+        out_specs=[VMEM] * 10,
+        out_shape=[pltpu.VMEM(*v) for v in shapes],
+        scratch_shapes=[pltpu.VMEM((8 * SLAB, L), jnp.float32), pltpu.SemaphoreType.DMA((8,))],
+        compiler_params=pltpu.CompilerParams(vmem_limit_bytes=16 << 20),
+        name="prepare",
+    )(*[far_off(v) for v in (w, t, own, *map(jnp.asarray, tables))])
+
+
+def late(chunks, prepared):
     return pl.pallas_call(
         late_kernel,
-        in_specs=[SMEM] + [ANY] * (4 + 16 - EARLY) + [VMEM] * 6,
-        out_shape=[f32(SLAB, L)] * 8,
+        in_specs=[VMEM] * 25,
+        out_specs=[VMEM] * 8,
+        out_shape=[pltpu.VMEM((SLAB, L), jnp.float32)] * 8,
         scratch_shapes=[
             pltpu.VMEM((N, N, L), jnp.float32),
             pltpu.VMEM((N * PITCH, L), jnp.float32),
             pltpu.VMEM((N * PITCH, L), jnp.float32),
-            pltpu.VMEM((H + 1, N, L), jnp.float32),
-            *near_scratch(16 - EARLY),
-            pltpu.SemaphoreType.DMA((2 * EARLY + 1,)),
             *HELD,
         ],
+        compiler_params=pltpu.CompilerParams(vmem_limit_bytes=24 << 20),
         name="late",
-    )(w, *chunks, t, s, one, k, *[jnp.asarray(v) for v in tables])
+    )(*[near(v) for v in chunks], *[near(v) for v in prepared])
 
 
 def tgt_move(value, dz, dy, dc):
@@ -373,8 +318,8 @@
     sent += [tgt_move(far, 1, 0, 0)]
     other = [tgt_move(v, 0, 0, 1) for v in sent]
     chunks = [v for both in zip(sent, other) for v in both]
-    s, one, k = early(chunks[:EARLY], t)
-    parts = late(occupations, chunks[EARLY:], t, s, one, k)
+    w, t, k, held, *tables = prepare(occupations, t, own)
+    parts = late([held, *chunks[1:]], (w, t, k, *tables))
 
     far = src_move(parts[0], 0, 1)
     up = src_move(parts[1], 1, 0)

time: 55.6 us -> 47.8 us (0.86)
  Pallas kernels: 13.5 us -> 7.65 us
  waiting for transfers between devices: 9.04 us -> 13.3 us
  other arithmetic: 3.47 us -> 0.73 us
  starting transfers between devices: 27.7 us -> 25.9 us
  local copies, waits for them, and re-layouts: 1.4 us -> 0 us
    pallas_call x2, Pallas kernels: 13.5 us -> 7.65 us  [the longest x1 4.62 us: late(): pl.pallas_call(late_kernel, in_specs=[VMEM] * 25, out_specs=[VMEM] * 8, o...]
    ppermute x15, waiting for transfers between devices: 6.72 us -> 8.94 us  [tgt_move(): return lax.ppermute(value, 'tgt', pairs)]
    ppermute x7, waiting for transfers between devices: 2.32 us -> 4.33 us  [src_move(): return lax.ppermute(value, 'src', pairs)]
    unnamed x30 -> x0, local copies, waits for them, and re-layouts: 1.4 us -> none
    ppermute x15, starting transfers between devices: 13.4 us -> 12.2 us  [tgt_move(): return lax.ppermute(value, 'tgt', pairs)]
    add x1, other arithmetic: 0.94 us -> 0.03 us  [on_device(): total = lax.optimization_barrier(sum(near, parts[7])) + crossed]
    add x1, other arithmetic: 0.93 us -> 0.02 us  [on_device(): crossed = src_move(parts[3] + up + down, 0, 1)]
    add x1, other arithmetic: 0.93 us -> 0.02 us  [on_device(): near.append(src_move(parts[4] + far, 2, 0))]
  transfers between devices with their start and end apart: 22 -> 22, of which waited for: 7 -> 8; matrix products, arithmetic and copies ran while one was open for 5% -> 0% of each run, Pallas kernels for 10% -> 6%
where the time goes in v1:
time: 47.8 us; the launch traced here: 47.7 us
  starting transfers between devices  25.9 us (54%)
  waiting for transfers between devices  13.3 us (28%)
  Pallas kernels  7.65 us (16%)
  other arithmetic  0.73 us (2%)
    ppermute x7, starting transfers between devices, src_move(): return lax.ppermute(value, 'src', pairs)  13.7 us
    ppermute x15, starting transfers between devices, tgt_move(): return lax.ppermute(value, 'tgt', pairs)  12.2 us
    ppermute x15, waiting for transfers between devices, tgt_move(): return lax.ppermute(value, 'tgt', pairs)  8.94 us
    pallas_call x1, Pallas kernels, late(): pl.pallas_call(late_kernel, in_specs=[VMEM] * 25, out_specs=[VMEM] * 8, o...  4.62 us
    ppermute x7, waiting for transfers between devices, src_move(): return lax.ppermute(value, 'src', pairs)  4.33 us
    pallas_call x1, Pallas kernels, prepare(): pl.pallas_call(prepare_kernel, in_specs=[SMEM] + [ANY] * 8, out_specs=[VM...  3.04 us
  transfers between devices with their start and end apart: 22, of which 8 were waited for; matrix products, arithmetic and copies ran while one was open for 0% of the time, Pallas kernels for 6%

profile of v1, /device:TPU:0, one launch (start us, length us, event | category | flops | bytes accessed | tf_op | source)
XLA Modules:
  0.0 47.7 jit_solution(17494314144704983800)
XLA Ops:
  0.0 3.1 %collective-permute-start.7 = (f32[256,128]{1,0:T(8,128)}, f32[256,128]{1,0:T(8,128)S(1)}, u32[]{:S(2)}, u32[]{:S(2)}) collective-permute-start(f32[256,128]{1,0:T(8,128)} %bitcast.17), channel_id=1, source_target_pairs={{0,48},{8,56},{16,0},{24,8},{32,16},{40,24},{48,32},{56,40},{64,11... | collective-permute-start | bytes 393224 | tf_op jit(solution)/shard_map/ppermute | solution.py:297
  3.1 2.2 %collective-permute-start.3 = (f32[256,128]{1,0:T(8,128)}, f32[256,128]{1,0:T(8,128)S(1)}, u32[]{:S(2)}, u32[]{:S(2)}) collective-permute-start(f32[256,128]{1,0:T(8,128)} %bitcast.19), channel_id=1, source_target_pairs={{0,32},{8,40},{16,48},{24,56},{32,0},{40,8},{48,16},{56,24},{64,96... | collective-permute-start | bytes 393224 | tf_op jit(solution)/shard_map/ppermute | solution.py:297
  5.3 1.9 %collective-permute-start.1 = (f32[256,128]{1,0:T(8,128)}, f32[256,128]{1,0:T(8,128)S(1)}, u32[]{:S(2)}, u32[]{:S(2)}) collective-permute-start(f32[256,128]{1,0:T(8,128)} %bitcast.20), channel_id=1, source_target_pairs={{0,64},{8,72},{16,80},{24,88},{32,96},{40,104},{48,112},{56,120},{... | collective-permute-start | bytes 393224 | tf_op jit(solution)/shard_map/ppermute | solution.py:297
  7.3 0.5 %collective-permute-start.8 = (f32[256,128]{1,0:T(8,128)S(1)}, f32[256,128]{1,0:T(8,128)S(1)}, u32[]{:S(2)}, u32[]{:S(2)}) collective-permute-start(f32[256,128]{1,0:T(8,128)S(1)} %collective-permute-done.7.refs_8_), channel_id=1, source_target_pairs={{0,8},{8,0},{16,24},{24,16},{32,40},{40,32},{48,56},{56,48},{64,72... | collective-permute-start | bytes 393224 | tf_op jit(solution)/shard_map/ppermute | solution.py:297
  7.8 4.5 %collective-permute-done.5.refs_6_ = f32[256,128]{1,0:T(8,128)S(1)} collective-permute-done((f32[256,128]{1,0:T(8,128)}, f32[256,128]{1,0:T(8,128)S(1)}, u32[]{:S(2)}, u32[]{:S(2)}) %collective-permute-start.5) | collective-permute-done | bytes 131104 | tf_op jit(solution)/shard_map/ppermute | solution.py:297
  12.3 1.9 %collective-permute-start.13 = (f32[256,128]{1,0:T(8,128)S(1)}, f32[256,128]{1,0:T(8,128)S(1)}, u32[]{:S(2)}, u32[]{:S(2)}) collective-permute-start(f32[256,128]{1,0:T(8,128)S(1)} %collective-permute-done.3.refs_4_), channel_id=1, source_target_pairs={{0,64},{8,72},{16,80},{24,88},{32,96},{40,104},{48,112},{56,120},{... | collective-permute-start | bytes 393224 | tf_op jit(solution)/shard_map/ppermute | solution.py:297
  14.2 0.7 %collective-permute-start.11 = (f32[256,128]{1,0:T(8,128)S(1)}, f32[256,128]{1,0:T(8,128)S(1)}, u32[]{:S(2)}, u32[]{:S(2)}) collective-permute-start(f32[256,128]{1,0:T(8,128)S(1)} %collective-permute-done.1.refs_2_), channel_id=1, source_target_pairs={{0,48},{8,56},{16,0},{24,8},{32,16},{40,24},{48,32},{56,40},{64,11... | collective-permute-start | bytes 393224 | tf_op jit(solution)/shard_map/ppermute | solution.py:297
  15.0 1.3 %collective-permute-start.9 = (f32[256,128]{1,0:T(8,128)S(1)}, f32[256,128]{1,0:T(8,128)S(1)}, u32[]{:S(2)}, u32[]{:S(2)}) collective-permute-start(f32[256,128]{1,0:T(8,128)S(1)} %collective-permute-done.1.refs_2_), channel_id=1, source_target_pairs={{0,16},{8,24},{16,32},{24,40},{32,48},{40,56},{48,0},{56,8},{64,80... | collective-permute-start | bytes 393224 | tf_op jit(solution)/shard_map/ppermute | solution.py:297
  16.8 1.6 %collective-permute-done.13.refs_14_ = f32[256,128]{1,0:T(8,128)S(1)} collective-permute-done((f32[256,128]{1,0:T(8,128)S(1)}, f32[256,128]{1,0:T(8,128)S(1)}, u32[]{:S(2)}, u32[]{:S(2)}) %collective-permute-start.13) | collective-permute-done | bytes 131104 | tf_op jit(solution)/shard_map/ppermute | solution.py:297
  18.4 1.5 %collective-permute-done.11.refs_12_ = f32[256,128]{1,0:T(8,128)S(1)} collective-permute-done((f32[256,128]{1,0:T(8,128)S(1)}, f32[256,128]{1,0:T(8,128)S(1)}, u32[]{:S(2)}, u32[]{:S(2)}) %collective-permute-start.11) | collective-permute-done | bytes 131104 | tf_op jit(solution)/shard_map/ppermute | solution.py:297
  19.9 1.3 %collective-permute-done.9.refs_10_ = f32[256,128]{1,0:T(8,128)S(1)} collective-permute-done((f32[256,128]{1,0:T(8,128)S(1)}, f32[256,128]{1,0:T(8,128)S(1)}, u32[]{:S(2)}, u32[]{:S(2)}) %collective-permute-start.9) | collective-permute-done | bytes 131104 | tf_op jit(solution)/shard_map/ppermute | solution.py:297
  21.2 3.0 %prepare.1 = (f32[8,128]{1,0:T(8,128)S(1)}, f32[64,64,128]{2,1,0:T(8,128)S(1)}, f32[33,64,128]{2,1,0:T(8,128)S(1)}, f32[256,128]{1,0:T(8,128)S(1)}, bf16[64,192]...) custom-call(f32[2]{0:T(128)} %w_ref.1, ...), custom_call_target="tpu_custom_call" | custom-call | tf_op jit(solution)/shard_map/prepare/pallas_call | solution.py:262
  24.3 4.6 %late.1 = (f32[256,128]{1,0:T(8,128)S(1)}, f32[256,128]{1,0:T(8,128)S(1)}, f32[256,128]{1,0:T(8,128)S(1)}, f32[256,128]{1,0:T(8,128)S(1)}, f32[256,128]{1,0:T(8,...) custom-call(f32[256,128]{1,0:T(8,128)S(1)} %get-tuple-element.23.refs_0_, ...), custom_call_target="tpu_custom_call" | custom-call | tf_op jit(solution)/shard_map/late/pallas_call | solution.py:274
  28.9 3.7 %collective-permute-start.17 = (f32[256,128]{1,0:T(8,128)S(1)}, f32[256,128]{1,0:T(8,128)S(1)}, u32[]{:S(2)}, u32[]{:S(2)}) collective-permute-start(f32[256,128]{1,0:T(8,128)S(1)} %get-tuple-element.37), channel_id=1, source_target_pairs={{0,1},{1,0},{2,3},{3,2},{4,5},{5,4},{6,7},{7,6},{8,9},{9,8},{10,11... | collective-permute-start | bytes 393224 | tf_op jit(solution)/shard_map/ppermute | solution.py:305
  32.6 1.5 %collective-permute-start.19 = (f32[256,128]{1,0:T(8,128)S(1)}, f32[256,128]{1,0:T(8,128)S(1)}, u32[]{:S(2)}, u32[]{:S(2)}) collective-permute-start(f32[256,128]{1,0:T(8,128)S(1)} %get-tuple-element.39), channel_id=1, source_target_pairs={{0,2},{1,3},{2,4},{3,5},{4,6},{5,7},{6,0},{7,1},{8,10},{9,11},{10,... | collective-permute-start | bytes 393224 | tf_op jit(solution)/shard_map/ppermute | solution.py:305
  34.0 1.7 %collective-permute-start.20 = (f32[256,128]{1,0:T(8,128)S(1)}, f32[256,128]{1,0:T(8,128)S(1)}, u32[]{:S(2)}, u32[]{:S(2)}) collective-permute-start(f32[256,128]{1,0:T(8,128)S(1)} %get-tuple-element.40), channel_id=1, source_target_pairs={{0,6},{1,7},{2,0},{3,1},{4,2},{5,3},{6,4},{7,5},{8,14},{9,15},{10,... | collective-permute-start | bytes 393224 | tf_op jit(solution)/shard_map/ppermute | solution.py:305
  36.1 3.0 %collective-permute-start.16 = (f32[256,128]{1,0:T(8,128)S(1)}, f32[256,128]{1,0:T(8,128)S(1)}, u32[]{:S(2)}, u32[]{:S(2)}) collective-permute-start(f32[256,128]{1,0:T(8,128)S(1)} %get-tuple-element.35), channel_id=1, source_target_pairs={{0,6},{1,7},{2,0},{3,1},{4,2},{5,3},{6,4},{7,5},{8,14},{9,15},{10,... | collective-permute-start | bytes 393224 | tf_op jit(solution)/shard_map/ppermute | solution.py:305
  39.1 0.8 %collective-permute-start.18 = (f32[256,128]{1,0:T(8,128)S(1)}, f32[256,128]{1,0:T(8,128)S(1)}, u32[]{:S(2)}, u32[]{:S(2)}) collective-permute-start(f32[256,128]{1,0:T(8,128)S(1)} %add.23), channel_id=1, source_target_pairs={{0,4},{1,5},{2,6},{3,7},{4,0},{5,1},{6,2},{7,3},{8,12},{9,13},{10,... | collective-permute-start | bytes 393224 | tf_op jit(solution)/shard_map/ppermute | solution.py:305
  39.9 0.6 %collective-permute-done.20 = f32[256,128]{1,0:T(8,128)S(1)} collective-permute-done((f32[256,128]{1,0:T(8,128)S(1)}, f32[256,128]{1,0:T(8,128)S(1)}, u32[]{:S(2)}, u32[]{:S(2)}) %collective-permute-start.20) | collective-permute-done | bytes 131104 | tf_op jit(solution)/shard_map/ppermute | solution.py:305
  40.4 2.8 %collective-permute-start.21 = (f32[256,128]{1,0:T(8,128)S(1)}, f32[256,128]{1,0:T(8,128)S(1)}, u32[]{:S(2)}, u32[]{:S(2)}) collective-permute-start(f32[256,128]{1,0:T(8,128)S(1)} %add_add_fusion), channel_id=1, source_target_pairs={{0,1},{1,0},{2,3},{3,2},{4,5},{5,4},{6,7},{7,6},{8,9},{9,8},{10,11... | collective-permute-start | bytes 393224 | tf_op jit(solution)/shard_map/ppermute | solution.py:305
  43.2 1.1 %collective-permute-done.16 = f32[256,128]{1,0:T(8,128)S(1)} collective-permute-done((f32[256,128]{1,0:T(8,128)S(1)}, f32[256,128]{1,0:T(8,128)S(1)}, u32[]{:S(2)}, u32[]{:S(2)}) %collective-permute-start.16) | collective-permute-done | bytes 131104 | tf_op jit(solution)/shard_map/ppermute | solution.py:305
  44.4 1.6 %collective-permute-done.18 = f32[256,128]{1,0:T(8,128)S(1)} collective-permute-done((f32[256,128]{1,0:T(8,128)S(1)}, f32[256,128]{1,0:T(8,128)S(1)}, u32[]{:S(2)}, u32[]{:S(2)}) %collective-permute-start.18) | collective-permute-done | bytes 131104 | tf_op jit(solution)/shard_map/ppermute | solution.py:305
  46.0 1.0 %collective-permute-done.21 = f32[256,128]{1,0:T(8,128)S(1)} collective-permute-done((f32[256,128]{1,0:T(8,128)S(1)}, f32[256,128]{1,0:T(8,128)S(1)}, u32[]{:S(2)}, u32[]{:S(2)}) %collective-permute-start.21) | collective-permute-done | bytes 131104 | tf_op jit(solution)/shard_map/ppermute | solution.py:305
  47.0 0.7 %add_bitcast_fusion = f32[1,8,4096]{2,1,0:T(8,128)} fusion(f32[256,128]{1,0:T(8,128)S(1)} %add_add_fusion.1, f32[256,128]{1,0:T(8,128)S(1)} %collective-permute-done.21), kind=kLoop, calls=%fused_computation | loop fusion | flops 32768 | bytes 393216 | tf_op jit(solution)/shard_map/reshape | solution.py:331
  (26 shorter events, 0.9 us)
Async XLA Ops:
  0.0 7.3 %collective-permute-start.7 = (f32[256,128]{1,0:T(8,128)}, f32[256,128]{1,0:T(8,128)S(1)}, u32[]{:S(2)}, u32[]{:S(2)}) collective-permute-start(f32[256,128]{1,0:T(8,128)} %bitcast.17), channel_id=1, source_target_pairs={{0,48},{8,56},{16,0},{24,8},{32,16},{40,24},{48,32},{56,40},{64,11... | collective-permute-start | bytes 393224 | tf_op jit(solution)/shard_map/ppermute | solution.py:297
  3.1 9.2 %collective-permute-start.5 = (f32[256,128]{1,0:T(8,128)}, f32[256,128]{1,0:T(8,128)S(1)}, u32[]{:S(2)}, u32[]{:S(2)}) collective-permute-start(f32[256,128]{1,0:T(8,128)} %bitcast.18), channel_id=1, source_target_pairs={{0,16},{8,24},{16,32},{24,40},{32,48},{40,56},{48,0},{56,8},{64,80... | collective-permute-start | bytes 393224 | tf_op jit(solution)/shard_map/ppermute | solution.py:297
  3.1 9.2 %collective-permute-start.3 = (f32[256,128]{1,0:T(8,128)}, f32[256,128]{1,0:T(8,128)S(1)}, u32[]{:S(2)}, u32[]{:S(2)}) collective-permute-start(f32[256,128]{1,0:T(8,128)} %bitcast.19), channel_id=1, source_target_pairs={{0,32},{8,40},{16,48},{24,56},{32,0},{40,8},{48,16},{56,24},{64,96... | collective-permute-start | bytes 393224 | tf_op jit(solution)/shard_map/ppermute | solution.py:297
  5.3 8.9 %collective-permute-start.1 = (f32[256,128]{1,0:T(8,128)}, f32[256,128]{1,0:T(8,128)S(1)}, u32[]{:S(2)}, u32[]{:S(2)}) collective-permute-start(f32[256,128]{1,0:T(8,128)} %bitcast.20), channel_id=1, source_target_pairs={{0,64},{8,72},{16,80},{24,88},{32,96},{40,104},{48,112},{56,120},{... | collective-permute-start | bytes 393224 | tf_op jit(solution)/shard_map/ppermute | solution.py:297
  7.3 7.7 %collective-permute-start = (f32[256,128]{1,0:T(8,128)}, f32[256,128]{1,0:T(8,128)S(1)}, u32[]{:S(2)}, u32[]{:S(2)}) collective-permute-start(f32[256,128]{1,0:T(8,128)} %bitcast.21), channel_id=1, source_target_pairs={{0,8},{8,0},{16,24},{24,16},{32,40},{40,32},{48,56},{56,48},{64,72... | collective-permute-start | bytes 393224 | tf_op jit(solution)/shard_map/ppermute | solution.py:297
  7.3 9.0 %collective-permute-start.8 = (f32[256,128]{1,0:T(8,128)S(1)}, f32[256,128]{1,0:T(8,128)S(1)}, u32[]{:S(2)}, u32[]{:S(2)}) collective-permute-start(f32[256,128]{1,0:T(8,128)S(1)} %collective-permute-done.7.refs_8_), channel_id=1, source_target_pairs={{0,8},{8,0},{16,24},{24,16},{32,40},{40,32},{48,56},{56,48},{64,72... | collective-permute-start | bytes 393224 | tf_op jit(solution)/shard_map/ppermute | solution.py:297
  12.3 4.0 %collective-permute-start.6 = (f32[256,128]{1,0:T(8,128)S(1)}, f32[256,128]{1,0:T(8,128)S(1)}, u32[]{:S(2)}, u32[]{:S(2)}) collective-permute-start(f32[256,128]{1,0:T(8,128)S(1)} %collective-permute-done.5.refs_6_), channel_id=1, source_target_pairs={{0,8},{8,0},{16,24},{24,16},{32,40},{40,32},{48,56},{56,48},{64,72... | collective-permute-start | bytes 393224 | tf_op jit(solution)/shard_map/ppermute | solution.py:297
  12.3 6.1 %collective-permute-start.13 = (f32[256,128]{1,0:T(8,128)S(1)}, f32[256,128]{1,0:T(8,128)S(1)}, u32[]{:S(2)}, u32[]{:S(2)}) collective-permute-start(f32[256,128]{1,0:T(8,128)S(1)} %collective-permute-done.3.refs_4_), channel_id=1, source_target_pairs={{0,64},{8,72},{16,80},{24,88},{32,96},{40,104},{48,112},{56,120},{... | collective-permute-start | bytes 393224 | tf_op jit(solution)/shard_map/ppermute | solution.py:297
  14.2 5.6 %collective-permute-start.11 = (f32[256,128]{1,0:T(8,128)S(1)}, f32[256,128]{1,0:T(8,128)S(1)}, u32[]{:S(2)}, u32[]{:S(2)}) collective-permute-start(f32[256,128]{1,0:T(8,128)S(1)} %collective-permute-done.1.refs_2_), channel_id=1, source_target_pairs={{0,48},{8,56},{16,0},{24,8},{32,16},{40,24},{48,32},{56,40},{64,11... | collective-permute-start | bytes 393224 | tf_op jit(solution)/shard_map/ppermute | solution.py:297
  15.0 6.2 %collective-permute-start.9 = (f32[256,128]{1,0:T(8,128)S(1)}, f32[256,128]{1,0:T(8,128)S(1)}, u32[]{:S(2)}, u32[]{:S(2)}) collective-permute-start(f32[256,128]{1,0:T(8,128)S(1)} %collective-permute-done.1.refs_2_), channel_id=1, source_target_pairs={{0,16},{8,24},{16,32},{24,40},{32,48},{40,56},{48,0},{56,8},{64,80... | collective-permute-start | bytes 393224 | tf_op jit(solution)/shard_map/ppermute | solution.py:297
  16.3 7.9 %collective-permute-start.4 = (f32[256,128]{1,0:T(8,128)S(1)}, f32[256,128]{1,0:T(8,128)S(1)}, u32[]{:S(2)}, u32[]{:S(2)}) collective-permute-start(f32[256,128]{1,0:T(8,128)S(1)} %collective-permute-done.3.refs_4_), channel_id=1, source_target_pairs={{0,8},{8,0},{16,24},{24,16},{32,40},{40,32},{48,56},{56,48},{64,72... | collective-permute-start | bytes 393224 | tf_op jit(solution)/shard_map/ppermute | solution.py:297
  16.3 7.9 %collective-permute-start.2 = (f32[256,128]{1,0:T(8,128)S(1)}, f32[256,128]{1,0:T(8,128)S(1)}, u32[]{:S(2)}, u32[]{:S(2)}) collective-permute-start(f32[256,128]{1,0:T(8,128)S(1)} %collective-permute-done.1.refs_2_), channel_id=1, source_target_pairs={{0,8},{8,0},{16,24},{24,16},{32,40},{40,32},{48,56},{56,48},{64,72... | collective-permute-start | bytes 393224 | tf_op jit(solution)/shard_map/ppermute | solution.py:297
  18.4 5.8 %collective-permute-start.14 = (f32[256,128]{1,0:T(8,128)S(1)}, f32[256,128]{1,0:T(8,128)S(1)}, u32[]{:S(2)}, u32[]{:S(2)}) collective-permute-start(f32[256,128]{1,0:T(8,128)S(1)} %collective-permute-done.13.refs_14_), channel_id=1, source_target_pairs={{0,8},{8,0},{16,24},{24,16},{32,40},{40,32},{48,56},{56,48},{64,72... | collective-permute-start | bytes 393224 | tf_op jit(solution)/shard_map/ppermute | solution.py:297
  19.9 4.4 %collective-permute-start.12 = (f32[256,128]{1,0:T(8,128)S(1)}, f32[256,128]{1,0:T(8,128)S(1)}, u32[]{:S(2)}, u32[]{:S(2)}) collective-permute-start(f32[256,128]{1,0:T(8,128)S(1)} %collective-permute-done.11.refs_12_), channel_id=1, source_target_pairs={{0,8},{8,0},{16,24},{24,16},{32,40},{40,32},{48,56},{56,48},{64,72... | collective-permute-start | bytes 393224 | tf_op jit(solution)/shard_map/ppermute | solution.py:297
  21.2 3.1 %collective-permute-start.10 = (f32[256,128]{1,0:T(8,128)S(1)}, f32[256,128]{1,0:T(8,128)S(1)}, u32[]{:S(2)}, u32[]{:S(2)}) collective-permute-start(f32[256,128]{1,0:T(8,128)S(1)} %collective-permute-done.9.refs_10_), channel_id=1, source_target_pairs={{0,8},{8,0},{16,24},{24,16},{32,40},{40,32},{48,56},{56,48},{64,72... | collective-permute-start | bytes 393224 | tf_op jit(solution)/shard_map/ppermute | solution.py:297
  28.9 10.2 %collective-permute-start.17 = (f32[256,128]{1,0:T(8,128)S(1)}, f32[256,128]{1,0:T(8,128)S(1)}, u32[]{:S(2)}, u32[]{:S(2)}) collective-permute-start(f32[256,128]{1,0:T(8,128)S(1)} %get-tuple-element.37), channel_id=1, source_target_pairs={{0,1},{1,0},{2,3},{3,2},{4,5},{5,4},{6,7},{7,6},{8,9},{9,8},{10,11... | collective-permute-start | bytes 393224 | tf_op jit(solution)/shard_map/ppermute | solution.py:305
  32.6 7.3 %collective-permute-start.19 = (f32[256,128]{1,0:T(8,128)S(1)}, f32[256,128]{1,0:T(8,128)S(1)}, u32[]{:S(2)}, u32[]{:S(2)}) collective-permute-start(f32[256,128]{1,0:T(8,128)S(1)} %get-tuple-element.39), channel_id=1, source_target_pairs={{0,2},{1,3},{2,4},{3,5},{4,6},{5,7},{6,0},{7,1},{8,10},{9,11},{10,... | collective-permute-start | bytes 393224 | tf_op jit(solution)/shard_map/ppermute | solution.py:305
  34.0 6.4 %collective-permute-start.20 = (f32[256,128]{1,0:T(8,128)S(1)}, f32[256,128]{1,0:T(8,128)S(1)}, u32[]{:S(2)}, u32[]{:S(2)}) collective-permute-start(f32[256,128]{1,0:T(8,128)S(1)} %get-tuple-element.40), channel_id=1, source_target_pairs={{0,6},{1,7},{2,0},{3,1},{4,2},{5,3},{6,4},{7,5},{8,14},{9,15},{10,... | collective-permute-start | bytes 393224 | tf_op jit(solution)/shard_map/ppermute | solution.py:305
  35.8 7.4 %collective-permute-start.15 = (f32[256,128]{1,0:T(8,128)S(1)}, f32[256,128]{1,0:T(8,128)S(1)}, u32[]{:S(2)}, u32[]{:S(2)}) collective-permute-start(f32[256,128]{1,0:T(8,128)S(1)} %get-tuple-element.34), channel_id=1, source_target_pairs={{0,2},{1,3},{2,4},{3,5},{4,6},{5,7},{6,0},{7,1},{8,10},{9,11},{10,... | collective-permute-start | bytes 393224 | tf_op jit(solution)/shard_map/ppermute | solution.py:305
  36.1 8.3 %collective-permute-start.16 = (f32[256,128]{1,0:T(8,128)S(1)}, f32[256,128]{1,0:T(8,128)S(1)}, u32[]{:S(2)}, u32[]{:S(2)}) collective-permute-start(f32[256,128]{1,0:T(8,128)S(1)} %get-tuple-element.35), channel_id=1, source_target_pairs={{0,6},{1,7},{2,0},{3,1},{4,2},{5,3},{6,4},{7,5},{8,14},{9,15},{10,... | collective-permute-start | bytes 393224 | tf_op jit(solution)/shard_map/ppermute | solution.py:305
  39.1 6.9 %collective-permute-start.18 = (f32[256,128]{1,0:T(8,128)S(1)}, f32[256,128]{1,0:T(8,128)S(1)}, u32[]{:S(2)}, u32[]{:S(2)}) collective-permute-start(f32[256,128]{1,0:T(8,128)S(1)} %add.23), channel_id=1, source_target_pairs={{0,4},{1,5},{2,6},{3,7},{4,0},{5,1},{6,2},{7,3},{8,12},{9,13},{10,... | collective-permute-start | bytes 393224 | tf_op jit(solution)/shard_map/ppermute | solution.py:305
  40.4 6.6 %collective-permute-start.21 = (f32[256,128]{1,0:T(8,128)S(1)}, f32[256,128]{1,0:T(8,128)S(1)}, u32[]{:S(2)}, u32[]{:S(2)}) collective-permute-start(f32[256,128]{1,0:T(8,128)S(1)} %add_add_fusion), channel_id=1, source_target_pairs={{0,1},{1,0},{2,3},{3,2},{4,5},{5,4},{6,7},{7,6},{8,9},{9,8},{10,11... | collective-permute-start | bytes 393224 | tf_op jit(solution)/shard_map/ppermute | solution.py:305
